TPU v7x, 128 devices: a whole 4x4x4 slice. The times are simulated.
128 devices in a mesh: feat: 4 (over z), trainer: 32 (over x, y, core).
Axes of the slice: x: 4, y: 4, z: 4, core: 2. Of those that a mesh axis runs over, the one named last changes fastest.
Arguments:
- features: bfloat16 [128, 131072], P('feat', 'trainer'), may hold values from -6 to 6
- first_adjacent: int32 [65536, 15], P('trainer'), may hold values from 0 to 4095
- first_center: int32 [65536], P('trainer'), may hold values from 0 to 4095
- first_count: int32 [65536], P('trainer'), may hold values from 1 to 15
- owner_map: int32 [65536], P('trainer'), may hold values from 0 to 127, as said below
- first_root: bfloat16 [128, 1024], P('feat'), may hold values from -0.5 to 0.5
- first_near: bfloat16 [128, 1024], P('feat'), may hold values from -0.5 to 0.5
- first_bias: float32 [1024], replicated, may hold values from -3 to 3
- second_adjacent: int32 [65536, 10], P(('feat', 'trainer')), may hold values from 0 to 1023, as said below
- second_center: int32 [65536], P(('feat', 'trainer')), may hold values from 0 to 1023, as said below
- second_count: int32 [65536], P(('feat', 'trainer')), may hold values from 1 to 10
- second_root: bfloat16 [1024, 1024], replicated, may hold values from -0.1875 to 0.1875
- second_near: bfloat16 [1024, 1024], replicated, may hold values from -0.1875 to 0.1875
- second_bias: float32 [1024], replicated, may hold values from -3 to 3
- upstream: bfloat16 [65536, 1024], P(('feat', 'trainer')), may hold values from -0.0234375 to 0.0234375
Outputs:
- layer_output: bfloat16 [65536, 1024], P(('feat', 'trainer'))
- rootgrad_two: float32 [1024, 1024], replicated
- neargrad_two: float32 [1024, 1024], replicated
- biasgrad_two: float32 [1024], replicated
- rootgrad_one: float32 [128, 1024], P('feat')
- neargrad_one: float32 [128, 1024], P('feat')
- biasgrad_one: float32 [1024], replicated
Inputs may be any that keep to these rules, and one draw needn't show every extreme that they name: `owner_map`: among the 2048 layer-one nodes of one trainer block at most 32 name any one owner; in every draw some owner is named by exactly 32 nodes of every block, and every owner is named by some node. `second_adjacent`: every entry names a filled row of the owner's table: row s * 32 + c with c smaller than the number of nodes of block s that name this owner. `second_center`: every entry names a filled row of the owner's table, as for second_adjacent.
All inputs are finite; a program needn't handle non-finite values.
Results may differ from a plain program's by a relative error of at most 0.025.
Values may be sent and summed in bfloat16 or wider, within the bound.
No kernel may reach another device: no remote copies, remote signals or barrier semaphores. Data moves between devices by JAX's collectives and lax.ppermute only.
A program may use at most 128 MiB of HBM per device.

v0:
```python
import jax
import jax.numpy as jnp
from jax import lax
from jax.sharding import PartitionSpec as P

CAP = 32


def in_one_piece(arrays, axis, dim, along):
    widths = [a.shape[along] for a in arrays]
    both = jnp.concatenate(arrays, axis=along)
    out = lax.all_gather(both, axis, axis=dim, tiled=True)
    return tuple(jnp.split(out, [sum(widths[:k]) for k in range(1, len(widths))], axis=along))


def in_one(arrays, axis):
    vector, at, finished = (jnp.concatenate([a.reshape(-1) for a in arrays]), 0, [])
    subtotal = lax.psum(vector, axis)
    for a in arrays:
        finished.append(subtotal[at : at + a.size].reshape(a.shape))
        at += a.size
    return tuple(finished)


def cross_rows(left, right):
    return lax.dot_general(
        left, right, (((0,), (0,)), ((), ())), preferred_element_type=jnp.float32
    )


def cross_cols(left, right):
    return lax.dot_general(
        left, right, (((1,), (1,)), ((), ())), preferred_element_type=jnp.float32
    )


def local(
    features,
    first_adjacent,
    first_center,
    first_count,
    owner_map,
    first_root,
    first_near,
    first_bias,
    second_adjacent,
    second_center,
    second_count,
    second_root,
    second_near,
    second_bias,
    upstream,
):
    feat_size = lax.axis_size("feat")
    trainers = lax.axis_size("trainer")
    owners_all = feat_size * trainers
    node_count = owner_map.shape[0]
    hidden_width = first_root.shape[1]
    block_width = features.shape[0]
    input_count = features.shape[1]
    fanout = first_adjacent.shape[1]
    slot_total = owners_all * CAP
    slots = trainers * CAP
    onehot = (owner_map[:, None] == jnp.arange(owners_all, dtype=jnp.int32)[None, :]).astype(
        jnp.int32
    )
    slot_rank = jnp.sum((jnp.cumsum(onehot, axis=0) - onehot) * onehot, axis=1)
    slot_node = (
        jnp.full((slot_total,), node_count, jnp.int32)
        .at[owner_map * CAP + slot_rank]
        .set(jnp.arange(node_count, dtype=jnp.int32))
    )
    filled = slot_node < node_count
    slot_adjacent = jnp.take(first_adjacent, slot_node, axis=0, mode="clip")
    slot_own = jnp.take(first_center, slot_node, axis=0, mode="clip")
    slot_count = jnp.where(filled, jnp.take(first_count, slot_node, axis=0, mode="clip"), 1)
    block_size = 512
    block_total = slot_total // block_size
    input_ids = jnp.arange(input_count, dtype=jnp.int32)[:, None]

    def select_block(pieces):
        adjacent_block, own_block, count_block, filled_block = pieces
        multiples = jnp.zeros((input_count, block_size), jnp.float32)
        for column in range(fanout):
            hits = (input_ids == adjacent_block[None, :, column]) & (
                (column < count_block) & filled_block
            )[None, :]
            multiples = multiples + jnp.where(hits, jnp.float32(1.0), jnp.float32(0.0))
        own_pick = ((input_ids == own_block[None, :]) & filled_block[None, :]).astype(jnp.bfloat16)
        own_cols = jnp.dot(features, own_pick, preferred_element_type=jnp.float32).astype(
            jnp.bfloat16
        )
        near_sum = jnp.dot(
            features, multiples.astype(jnp.bfloat16), preferred_element_type=jnp.float32
        )
        near_cols = (near_sum / count_block.astype(jnp.float32)[None, :]).astype(jnp.bfloat16)
        return (own_cols, near_cols)

    blocks_in = (
        slot_adjacent.reshape(block_total, block_size, fanout),
        slot_own.reshape(block_total, block_size),
        slot_count.reshape(block_total, block_size),
        filled.reshape(block_total, block_size),
    )
    own_blocks, near_blocks = lax.map(select_block, blocks_in)
    slot_center = own_blocks.transpose(1, 0, 2).reshape(block_width, slot_total)
    slot_near = near_blocks.transpose(1, 0, 2).reshape(block_width, slot_total)
    packed = jnp.stack([slot_center, slot_near]).reshape(2, block_width, owners_all, CAP)
    arrived = lax.all_to_all(packed, ("feat", "trainer"), split_axis=2, concat_axis=2, tiled=True)
    arrived = (
        arrived.reshape(2, block_width, feat_size, trainers, CAP)
        .transpose(0, 2, 1, 3, 4)
        .reshape(2, feat_size * block_width, slots)
    )
    owner_center = arrived[0]
    owner_near = arrived[1]
    root_all, near_all = in_one_piece((first_root, first_near), "feat", 0, 1)
    pre_one = jnp.zeros((slots, hidden_width), jnp.float32) + first_bias
    for quarter in range(feat_size):
        low = quarter * block_width
        high = low + block_width
        part = cross_rows(owner_center[low:high], root_all[low:high]) + cross_rows(
            owner_near[low:high], near_all[low:high]
        )
        pre_one = pre_one + part.astype(jnp.bfloat16).astype(jnp.float32)
    hidden_table = jax.nn.softplus(pre_one).astype(jnp.bfloat16)
    slot_ids = jnp.arange(slots, dtype=jnp.int32)
    root_pick = (second_center[:, None] == slot_ids[None, :]).astype(jnp.bfloat16)
    root_rows = jnp.dot(root_pick, hidden_table, preferred_element_type=jnp.float32).astype(
        jnp.bfloat16
    )
    multiples = jnp.zeros((second_center.shape[0], slots), jnp.float32)
    for column in range(second_adjacent.shape[1]):
        hits = (column < second_count)[:, None] & (
            second_adjacent[:, column : column + 1] == slot_ids[None, :]
        )
        multiples = multiples + jnp.where(hits, jnp.float32(1.0), jnp.float32(0.0))
    multiples = multiples.astype(jnp.bfloat16)
    divisor = second_count.astype(jnp.float32)[:, None]
    near_two = (
        jnp.dot(multiples, hidden_table, preferred_element_type=jnp.float32) / divisor
    ).astype(jnp.bfloat16)
    pre_two = jnp.dot(root_rows, second_root, preferred_element_type=jnp.float32)
    pre_two = (
        pre_two + jnp.dot(near_two, second_near, preferred_element_type=jnp.float32) + second_bias
    )
    gate = jax.nn.sigmoid(pre_two)
    layer_output = (pre_two * gate).astype(jnp.bfloat16)
    slope_two = (upstream.astype(jnp.float32) * gate * (1.0 + pre_two * (1.0 - gate))).astype(
        jnp.bfloat16
    )
    rootgrad_two, neargrad_two, biasgrad_two = lax.psum(
        (
            cross_rows(root_rows, slope_two),
            cross_rows(near_two, slope_two),
            jnp.sum(slope_two.astype(jnp.float32), axis=0),
        ),
        ("feat", "trainer"),
    )
    back_root = cross_cols(slope_two, second_root).astype(jnp.bfloat16)
    back_near = (cross_cols(slope_two, second_near) / divisor).astype(jnp.bfloat16)
    table_grad = cross_rows(root_pick, back_root) + cross_rows(multiples, back_near)
    pre_grad = (table_grad * (1.0 - jnp.exp(-hidden_table.astype(jnp.float32)))).astype(
        jnp.bfloat16
    )
    root_full = jnp.dot(owner_center, pre_grad, preferred_element_type=jnp.float32)
    near_full = jnp.dot(owner_near, pre_grad, preferred_element_type=jnp.float32)
    bias_full = jnp.sum(pre_grad.astype(jnp.float32), axis=0)
    root_sum, near_sum, biasgrad_one = in_one(
        (root_full, near_full, bias_full), ("feat", "trainer")
    )
    offset = lax.axis_index("feat") * block_width
    rootgrad_one = lax.dynamic_slice_in_dim(root_sum, offset, block_width, 0)
    neargrad_one = lax.dynamic_slice_in_dim(near_sum, offset, block_width, 0)
    return (
        layer_output,
        rootgrad_two,
        neargrad_two,
        biasgrad_two,
        rootgrad_one,
        neargrad_one,
        biasgrad_one,
    )


def solution(mesh):
    return jax.shard_map(
        local,
        mesh=mesh,
        in_specs=(
            P("feat", "trainer"),
            P("trainer", None),
            P("trainer"),
            P("trainer"),
            P("trainer"),
            P("feat", None),
            P("feat", None),
            P(),
            P(("feat", "trainer"), None),
            P(("feat", "trainer")),
            P(("feat", "trainer")),
            P(),
            P(),
            P(),
            P(("feat", "trainer"), None),
        ),
        out_specs=(
            P(("feat", "trainer"), None),
            P(),
            P(),
            P(),
            P("feat", None),
            P("feat", None),
            P(),
        ),
        check_vma=False,
    )
```

profile of v0, /device:TPU:1, one launch (start us, length us, event | category | flops | bytes accessed | tf_op | source)
XLA Modules:
  0.0 660.4 jit_solution(13970809639460819845)
XLA Ops:
  9.9 8.1 %scatter_custom_fusion = s32[4096]{0:T(1024)S(1)} fusion(s32[2048]{0:T(1024)S(1)} %compare_select_fusion.1, s32[2048]{0:T(1024)S(1)} %iota.50, s32[]{:T(128)} %constant.15.clone.1), kind=kCustom, calls=%fused_computation.160 | custom fusion | bytes 16388 | tf_op jit(solution)/shard_map/scatter | solution.py:71
  18.0 23.0 %gather_fusion.2 = s32[4096]{0:T(1024)S(1)} fusion(s32[2048]{0:T(1024)S(1)} %copy-done.1, s32[4096]{0:T(1024)S(1)} %broadcast_clamp_fusion), kind=kCustom, calls=%fused_computation.2 | custom fusion | bytes 49152 | tf_op jit(solution)/shard_map/jit(_take)/gather | solution.py:76
  41.5 14.2 %gather_fusion.1 = s32[4096,15]{1,0:T(8,128)} fusion(s32[2048,15]{1,0:T(8,128)S(1)} %copy.43, s32[4096]{0:T(1024)S(1)} %broadcast_clamp_fusion), kind=kCustom, calls=%fused_computation.1 | custom fusion | bytes 507904 | tf_op jit(solution)/shard_map/jit(_take)/gather | solution.py:74
  55.7 2.2 copy.44
  57.9 23.0 %gather_fusion = s32[4096]{0:T(1024)S(1)} fusion(s32[2048]{0:T(1024)S(1)} %copy-done.2, s32[4096]{0:T(1024)S(1)} %broadcast_clamp_fusion), kind=kCustom, calls=%fused_computation | custom fusion | bytes 49152 | tf_op jit(solution)/shard_map/jit(_take)/gather | solution.py:75
  81.0 254.4 %while.14 = (s32[]{:T(128)}, bf16[8,32,512]{2,1,0:T(8,128)(2,1)}, bf16[8,32,512]{2,1,0:T(8,128)(2,1)}, s32[8,512]{1,0:T(8,128)S(1)}, pred[8,512]{1,0:T(8,128)(4,...) while((s32[]{:T(128)}, bf16[8,32,512]{2,1,0:T(8,128)(2,1)}, ...), condition=%wide.region_5.6_spmd.clone.clone, body=%wide.region_4.5_spmd.clone.clone.sunk | while | flops 398523904 | bytes 777833 | solution.py:105
  81.5 27.7 %fusion.138 = bf16[8,32,512]{2,1,0:T(8,128)(2,1)} fusion(bf16[8,32,512]{2,1,0:T(8,128)(2,1)} %get-tuple-element.410, s32[]{:T(128)} %get-tuple-element.408, bf16[32,4096]{1,0:T(8,128)(2,1)S(1)} %get-tuple-element.422, s32[512]{0:T(512)S(1)} %bitcast.172, s32[512]{0:T(512)S(1)} %bitcast.173, s32[512]{0:T(512)S(1)} %bitcast.174, ...), kind=kOutput, calls=%fused_computation.63.clone.1 | convolution fusion | flops 260079616 | bytes 335872 | tf_op jit(solution)/shard_map/while/body/eval_jaxpr/dot_general | solution.py:93
  109.2 2.3 fusion.136
  111.7 27.7 %fusion.138 = bf16[8,32,512]{2,1,0:T(8,128)(2,1)} fusion(bf16[8,32,512]{2,1,0:T(8,128)(2,1)} %get-tuple-element.410, s32[]{:T(128)} %get-tuple-element.408, bf16[32,4096]{1,0:T(8,128)(2,1)S(1)} %get-tuple-element.422, s32[512]{0:T(512)S(1)} %bitcast.172, s32[512]{0:T(512)S(1)} %bitcast.173, s32[512]{0:T(512)S(1)} %bitcast.174, ...), kind=kOutput, calls=%fused_computation.63.clone.1 | convolution fusion | flops 260079616 | bytes 335872 | tf_op jit(solution)/shard_map/while/body/eval_jaxpr/dot_general | solution.py:93
  139.4 2.3 fusion.136
  141.9 27.7 %fusion.138 = bf16[8,32,512]{2,1,0:T(8,128)(2,1)} fusion(bf16[8,32,512]{2,1,0:T(8,128)(2,1)} %get-tuple-element.410, s32[]{:T(128)} %get-tuple-element.408, bf16[32,4096]{1,0:T(8,128)(2,1)S(1)} %get-tuple-element.422, s32[512]{0:T(512)S(1)} %bitcast.172, s32[512]{0:T(512)S(1)} %bitcast.173, s32[512]{0:T(512)S(1)} %bitcast.174, ...), kind=kOutput, calls=%fused_computation.63.clone.1 | convolution fusion | flops 260079616 | bytes 335872 | tf_op jit(solution)/shard_map/while/body/eval_jaxpr/dot_general | solution.py:93
  169.6 2.3 fusion.136
  172.1 27.7 %fusion.138 = bf16[8,32,512]{2,1,0:T(8,128)(2,1)} fusion(bf16[8,32,512]{2,1,0:T(8,128)(2,1)} %get-tuple-element.410, s32[]{:T(128)} %get-tuple-element.408, bf16[32,4096]{1,0:T(8,128)(2,1)S(1)} %get-tuple-element.422, s32[512]{0:T(512)S(1)} %bitcast.172, s32[512]{0:T(512)S(1)} %bitcast.173, s32[512]{0:T(512)S(1)} %bitcast.174, ...), kind=kOutput, calls=%fused_computation.63.clone.1 | convolution fusion | flops 260079616 | bytes 335872 | tf_op jit(solution)/shard_map/while/body/eval_jaxpr/dot_general | solution.py:93
  199.8 2.3 fusion.136
  202.3 27.7 %fusion.138 = bf16[8,32,512]{2,1,0:T(8,128)(2,1)} fusion(bf16[8,32,512]{2,1,0:T(8,128)(2,1)} %get-tuple-element.410, s32[]{:T(128)} %get-tuple-element.408, bf16[32,4096]{1,0:T(8,128)(2,1)S(1)} %get-tuple-element.422, s32[512]{0:T(512)S(1)} %bitcast.172, s32[512]{0:T(512)S(1)} %bitcast.173, s32[512]{0:T(512)S(1)} %bitcast.174, ...), kind=kOutput, calls=%fused_computation.63.clone.1 | convolution fusion | flops 260079616 | bytes 335872 | tf_op jit(solution)/shard_map/while/body/eval_jaxpr/dot_general | solution.py:93
  230.0 2.3 fusion.136
  232.4 27.7 %fusion.138 = bf16[8,32,512]{2,1,0:T(8,128)(2,1)} fusion(bf16[8,32,512]{2,1,0:T(8,128)(2,1)} %get-tuple-element.410, s32[]{:T(128)} %get-tuple-element.408, bf16[32,4096]{1,0:T(8,128)(2,1)S(1)} %get-tuple-element.422, s32[512]{0:T(512)S(1)} %bitcast.172, s32[512]{0:T(512)S(1)} %bitcast.173, s32[512]{0:T(512)S(1)} %bitcast.174, ...), kind=kOutput, calls=%fused_computation.63.clone.1 | convolution fusion | flops 260079616 | bytes 335872 | tf_op jit(solution)/shard_map/while/body/eval_jaxpr/dot_general | solution.py:93
  260.1 2.3 fusion.136
  262.6 27.7 %fusion.138 = bf16[8,32,512]{2,1,0:T(8,128)(2,1)} fusion(bf16[8,32,512]{2,1,0:T(8,128)(2,1)} %get-tuple-element.410, s32[]{:T(128)} %get-tuple-element.408, bf16[32,4096]{1,0:T(8,128)(2,1)S(1)} %get-tuple-element.422, s32[512]{0:T(512)S(1)} %bitcast.172, s32[512]{0:T(512)S(1)} %bitcast.173, s32[512]{0:T(512)S(1)} %bitcast.174, ...), kind=kOutput, calls=%fused_computation.63.clone.1 | convolution fusion | flops 260079616 | bytes 335872 | tf_op jit(solution)/shard_map/while/body/eval_jaxpr/dot_general | solution.py:93
  290.3 2.3 fusion.136
  292.8 27.7 %fusion.138 = bf16[8,32,512]{2,1,0:T(8,128)(2,1)} fusion(bf16[8,32,512]{2,1,0:T(8,128)(2,1)} %get-tuple-element.410, s32[]{:T(128)} %get-tuple-element.408, bf16[32,4096]{1,0:T(8,128)(2,1)S(1)} %get-tuple-element.422, s32[512]{0:T(512)S(1)} %bitcast.172, s32[512]{0:T(512)S(1)} %bitcast.173, s32[512]{0:T(512)S(1)} %bitcast.174, ...), kind=kOutput, calls=%fused_computation.63.clone.1 | convolution fusion | flops 260079616 | bytes 335872 | tf_op jit(solution)/shard_map/while/body/eval_jaxpr/dot_general | solution.py:93
  320.5 2.3 fusion.136
  338.2 1.6 stack.8
  339.8 1.7 pad_maximum_fusion
  341.5 2.7 copy.54
  344.1 4.5 reshape.178
  348.6 11.5 %all-to-all-start = ((bf16[128,2,1024]{2,1,0:T(2,128)(2,1)}), bf16[128,2,1024]{2,1,0:T(2,128)(2,1)S(1)}, u32[]{:S(2)}, u32[]{:S(2)}) async-start(bf16[128,2,1024]{2,1,0:T(2,128)(2,1)} %reshape.178), calls=%async_computation | async-start | bytes 1048576 | tf_op jit(solution)/shard_map/all_to_all | solution.py:109
  360.2 15.7 %all_gather.3 = bf16[128,2048]{1,0:T(8,128)(2,1)} all-gather(bf16[32,2048]{1,0:T(8,128)(2,1)S(1)} %pad_maximum_fusion.2), channel_id=1, replica_groups=mesh['feat'=4,'trainer'=32] {'feat'}, dimensions={0}, use_global_device_ids=true | all-gather | bytes 655360 | tf_op jit(solution)/shard_map/all_gather | solution.py:12
  377.7 2.0 reshape.179
  379.7 2.9 copy.53
  382.7 1.3 fusion.91
  384.0 1.5 fusion.90
  385.5 1.2 slice.215
  386.7 1.2 slice.218
  388.0 1.9 slice.221
  389.8 3.5 fusion.81
  393.4 3.6 fusion.78
  398.2 1.9 slice.227
  400.0 3.6 fusion.75
  403.7 1.9 slice.230
  405.5 1.9 slice.209
  407.4 3.6 fusion.84
  411.9 3.1 add_convert_fusion.12
  415.3 1.7 add_convert_fusion.11
  417.6 1.7 add_convert_fusion.10
  419.8 4.4 fusion.53
  424.2 1.7 fusion.66
  426.7 1.3 fusion.94
  428.2 7.0 %divide_convert_fusion.1 = bf16[512,1024]{1,0:T(8,128)(2,1)S(1)} fusion(bf16[1024,1024]{1,0:T(8,128)(2,1)S(1)} %fusion.53, f32[512]{0:T(512)S(1)} %copy-done.27, s32[512]{0:T(512)S(1)} %bitcast.204, s32[512]{0:T(512)S(1)} %bitcast.206, s32[512]{0:T(512)S(1)} %bitcast.190, s32[512]{0:T(512)S(1)} %bitcast.192, s32[512]{0:T(512)S(1)} %bitcast.194, ...), kind=kOutput, calls=%fused_computation.101 | convolution fusion | flops 1095761920 | bytes 3173376 | tf_op jit(solution)/shard_map/dot_general | solution.py:141
  435.3 3.5 convert_reduce_fusion.1
  438.7 6.2 fusion.54
  444.9 5.0 fusion.96
  449.9 3.3 fusion.95
  453.3 11.6 %convert_reduce_fusion = (f32[1024]{0:T(1024)S(1)}, bf16[1024,1024]{1,0:T(8,128)(2,1)}) fusion(bf16[1024,1024]{1,0:T(8,128)(2,1)} %copy-done.44, f32[1024,1024]{1,0:T(8,128)} %fusion.54, bf16[512,1024]{1,0:T(8,128)(2,1)} %get-tuple-element.226, bf16[1024,1024]{1,0:T(8,128)(2,1)S(1)} %copy-done, f32[512]{0:T(512)S(1)} %copy-done.27, s32[512]{0:T(512)S(1)} %bitcast.205, ...), kind=kOutput, calls=%fused_computation.87 | convolution fusion | flops 2177891328 | bytes 11566080 | tf_op jit(solution)/shard_map/dot_general | solution.py:26
  464.8 2.3 squeeze.13
  467.2 2.0 convolution_bitcast_fusion.1
  471.2 2.1 convolution_bitcast_fusion
  474.5 67.6 %psum.30 = f32[1024]{0:T(1024)} all-reduce(f32[1024]{0:T(1024)S(1)} %get-tuple-element.225), channel_id=1, replica_groups=mesh['feat'=4,'trainer'=32] {'feat','trainer'}, use_global_device_ids=true, to_apply=%region_9.10 | all-reduce | flops 1024 | bytes 8192 | tf_op jit(solution)/shard_map/psum | solution.py:152
  542.1 99.2 %all-reduce.3.cloned.1.call-done = (f32[1024,1024]{1,0:T(8,128)}, f32[1024,1024]{1,0:T(8,128)}, f32[263168]{0:T(1024)}) async-done(((f32[1024,1024]{1,0:T(8,128)}, f32[1024,1024]{1,0:T(8,128)}, f32[263168]{0:T(1024)}), (f32[1024,1024]{1,0:T(8,128)}, f32[1024,1024]{1,0:T(8,128)}, f32[263168]{0:T(1024)})) %all-reduce.3.cloned.1.call-update) | async-done | bytes 9441296 | tf_op jit(solution)/shard_map/psum | solution.py:152
  641.3 1.3 fusion.92
  642.6 1.3 slice.322
  644.8 1.6 constant_dynamic-slice_fusion.3
  646.5 4.9 copy.69
  651.4 2.0 copy.70
  (158 shorter events, 17.3 us)
Async XLA Ops:
  7.2 428.1 %copy-start = (bf16[1024,1024]{1,0:T(8,128)(2,1)S(1)}, bf16[1024,1024]{1,0:T(8,128)(2,1)}, u32[]{:S(2)}) copy-start(bf16[1024,1024]{1,0:T(8,128)(2,1)} %param.29) | copy-start | bytes 6291460
  8.5 0.7 copy-start.15
  8.6 9.3 %copy-start.1 = (s32[2048]{0:T(1024)S(1)}, s32[2048]{0:T(1024)}, u32[]{:S(2)}) copy-start(s32[2048]{0:T(1024)} %param.20) | copy-start | bytes 24580
  18.0 23.1 %copy-start.14 = (s32[2048,15]{0,1:T(8,128)S(1)}, s32[2048,15]{0,1:T(8,128)}, u32[]{:S(2)}) copy-start(s32[2048,15]{0,1:T(8,128)} %param.18) | copy-start | bytes 368644
  55.7 2.2 copy-start.2
  57.9 23.1 %copy-start.40 = (bf16[32,4096]{1,0:T(8,128)(2,1)S(1)}, bf16[32,4096]{1,0:T(8,128)(2,1)}, u32[]{:S(2)}) copy-start(bf16[32,4096]{1,0:T(8,128)(2,1)} %param.17) | copy-start | bytes 786436
  344.1 16.0 %copy-start.17 = (bf16[32,1024]{1,0:T(8,128)(2,1)S(1)}, bf16[32,1024]{1,0:T(8,128)(2,1)}, u32[]{:S(2)}) copy-start(bf16[32,1024]{1,0:T(8,128)(2,1)} %param.23) | copy-start | bytes 196612
  344.1 16.0 %copy-start.18 = (bf16[32,1024]{1,0:T(8,128)(2,1)S(1)}, bf16[32,1024]{1,0:T(8,128)(2,1)}, u32[]{:S(2)}) copy-start(bf16[32,1024]{1,0:T(8,128)(2,1)} %param.22) | copy-start | bytes 196612
  344.1 31.8 %copy-start.20 = (s32[512]{0:T(512)S(1)}, s32[512]{0:T(512)}, u32[]{:S(2)}) copy-start(s32[512]{0:T(512)} %param.27) | copy-start | bytes 6148
  344.1 33.0 %copy-start.19 = (s32[512,10]{0,1:T(8,128)S(1)}, s32[512,10]{0,1:T(8,128)}, u32[]{:S(2)}) copy-start(s32[512,10]{0,1:T(8,128)} %param.25) | copy-start | bytes 61444
  348.6 29.1 %all-to-all-start = ((bf16[128,2,1024]{2,1,0:T(2,128)(2,1)}), bf16[128,2,1024]{2,1,0:T(2,128)(2,1)S(1)}, u32[]{:S(2)}, u32[]{:S(2)}) async-start(bf16[128,2,1024]{2,1,0:T(2,128)(2,1)} %reshape.178), calls=%async_computation | async-start | bytes 1048576 | tf_op jit(solution)/shard_map/all_to_all | solution.py:109
  360.1 281.2 %all-reduce.3.cloned.1.call-start = ((), (), s32[]{:S(2)}) async-start(), calls=%async_computation.1 | async-start | bytes 18882560 | tf_op jit(solution)/shard_map/psum | solution.py:152
  389.8 3.5 copy-start.13
  411.9 3.5 copy-start.3
  415.3 2.2 copy-start.4
  415.3 2.2 copy-start.12
  417.6 2.2 copy-start.6
  417.6 2.2 copy-start.16
  417.6 2.2 copy-start.41
  419.8 4.4 copy-start.43
  424.2 3.8 copy-start.44
  424.2 2.4 copy-start.38
  426.6 1.4 copy-start.9
  426.6 1.4 copy-start.21
  426.6 1.4 copy-start.22
  426.6 1.5 copy-start.23
  426.6 1.5 copy-start.24
  426.6 1.5 copy-start.25
  426.6 1.5 copy-start.26
  426.6 1.5 copy-start.27
  426.6 1.5 copy-start.28
  426.6 1.5 copy-start.29
  426.6 1.5 copy-start.30
  426.6 1.5 copy-start.31
  426.7 1.5 copy-start.32
  426.7 1.5 copy-start.33
  426.7 1.5 copy-start.34
  426.7 1.5 copy-start.35
  426.7 1.5 copy-start.36
  426.7 1.5 copy-start.37
  428.2 7.1 %copy-start.39 = (bf16[512,1024]{1,0:T(8,128)(2,1)S(1)}, bf16[512,1024]{1,0:T(8,128)(2,1)}, u32[]{:S(2)}) copy-start(bf16[512,1024]{1,0:T(8,128)(2,1)} %param.31) | copy-start | bytes 3145732
  428.2 7.1 %copy-start.42 = (f32[1024]{0:T(1024)S(1)}, f32[1024]{0:T(1024)}, u32[]{:S(2)}) copy-start(f32[1024]{0:T(1024)} %param.30) | copy-start | bytes 12292
  435.2 3.5 copy-start.11
  444.9 5.0 copy-start.7
  444.9 5.0 copy-start.10
  471.2 2.2 copy-start.8
  646.5 4.9 copy-start.5
Sparse Core Ops, SparseCore 0:
  474.6 166.6 all-reduce.2
where the time goes:
time: 665 us; the launch traced here: 660 us
  matrix products  309 us (46%)
  local copies, waits for them, and re-layouts  123 us (18%)
  waiting for transfers between devices  99.2 us (15%)
  blocking collectives  83.4 us (13%)
  between operations  15 us (2%)
  loops' own time  13.2 us (2%)
  starting transfers between devices  11.5 us (2%)
    dot_general x8, matrix products, select_block(): jnp.dot(features, multiples.astype(jnp.bfloat16), preferred_element_type=...  222 us
    psum x1, waiting for transfers between devices, local(): lax.psum((cross_rows(root_rows, slope_two), cross_rows(near_two, slope_tw...  99.2 us
    psum x1, blocking collectives, local(): lax.psum((cross_rows(root_rows, slope_two), cross_rows(near_two, slope_tw...  67.6 us
    dot_general x12, matrix products, cross_rows(): lax.dot_general(left, right, (((0,), (0,)), ((), ())), preferred_element_...  51.3 us
    gather x1, local copies, waits for them, and re-layouts, local(): slot_own = jnp.take(first_center, slot_node, axis=0, mode='clip')  23 us
    gather x1, local copies, waits for them, and re-layouts, local(): jnp.take(first_count, slot_node, axis=0, mode='clip')  23 us
    unnamed x98, local copies, waits for them, and re-layouts  19.4 us
    dot_general x8, matrix products, select_block(): jnp.dot(features, own_pick, preferred_element_type=jnp.float32)  18.4 us
  transfers between devices with their start and end apart: 2, of which 1 were waited for; matrix products, arithmetic and copies ran while one was open for 0% of the time, Pallas kernels for 0%

commit v1 on v0

--- a/solution.py
+++ b/solution.py
@@ -150,12 +150,15 @@
         jnp.bfloat16
     )
     rootgrad_two, neargrad_two, biasgrad_two = lax.psum(
-        (
-            cross_rows(root_rows, slope_two),
-            cross_rows(near_two, slope_two),
-            jnp.sum(slope_two.astype(jnp.float32), axis=0),
+        lax.psum(
+            (
+                cross_rows(root_rows, slope_two),
+                cross_rows(near_two, slope_two),
+                jnp.sum(slope_two.astype(jnp.float32), axis=0),
+            ),
+            "trainer",
         ),
-        ("feat", "trainer"),
+        "feat",
     )
     back_root = cross_cols(slope_two, second_root).astype(jnp.bfloat16)
     back_near = (cross_cols(slope_two, second_near) / divisor).astype(jnp.bfloat16)

time: 665 us -> 909 us (1.37)
  waiting for transfers between devices: 99.2 us -> 345 us
    psum x0 -> x2, waiting for transfers between devices: none -> 237 us  [the longest x1 156 us: local(): lax.psum(lax.psum((cross_rows(root_rows, slope_two), cross_rows(near_two,...]
    psum x0 -> x1, blocking collectives: none -> 9.53 us  [local(): lax.psum(lax.psum((cross_rows(root_rows, slope_two), cross_rows(near_two,...]
    unnamed x98 -> x96, local copies, waits for them, and re-layouts: 19.4 us -> 21.5 us
  transfers between devices with their start and end apart: 2 -> 4, of which waited for: 1 -> 3; matrix products, arithmetic and copies ran while one was open for 0% -> 2% of each run, Pallas kernels for 0% -> 0%
where the time goes in v1:
time: 909 us; the launch traced here: 905 us
  waiting for transfers between devices  345 us (38%)
  matrix products  303 us (33%)
  local copies, waits for them, and re-layouts  124 us (14%)
  blocking collectives  87.7 us (10%)
  between operations  14.7 us (2%)
  loops' own time  13.2 us (1%)
  starting transfers between devices  11.6 us (1%)
    dot_general x8, matrix products, select_block(): jnp.dot(features, multiples.astype(jnp.bfloat16), preferred_element_type=...  222 us
    psum x1, waiting for transfers between devices, local(): lax.psum(lax.psum((cross_rows(root_rows, slope_two), cross_rows(near_two,...  156 us
    psum x1, waiting for transfers between devices, local(): lax.psum((cross_rows(root_rows, slope_two), cross_rows(near_two, slope_tw...  108 us
    psum x1, waiting for transfers between devices, in_one(): subtotal = lax.psum(vector, axis)  80.4 us
    psum x1, blocking collectives, local(): lax.psum((cross_rows(root_rows, slope_two), cross_rows(near_two, slope_tw...  62.9 us
    dot_general x12, matrix products, cross_rows(): lax.dot_general(left, right, (((0,), (0,)), ((), ())), preferred_element_...  44.8 us
    gather x1, local copies, waits for them, and re-layouts, local(): slot_own = jnp.take(first_center, slot_node, axis=0, mode='clip')  23 us
    gather x1, local copies, waits for them, and re-layouts, local(): jnp.take(first_count, slot_node, axis=0, mode='clip')  23 us
  transfers between devices with their start and end apart: 4, of which 3 were waited for; matrix products, arithmetic and copies ran while one was open for 2% of the time, Pallas kernels for 0%

profile of v1, /device:TPU:1, one launch (start us, length us, event | category | flops | bytes accessed | tf_op | source)
XLA Modules:
  0.0 905.0 jit_solution(2341747962652245053)
XLA Ops:
  9.9 8.1 scatter_custom_fusion
  18.0 23.0 %gather_fusion.2 = s32[4096]{0:T(1024)S(1)} fusion(s32[2048]{0:T(1024)S(1)} %copy-done.1, s32[4096]{0:T(1024)S(1)} %broadcast_clamp_fusion), kind=kCustom, calls=%fused_computation.2 | custom fusion | bytes 49152 | tf_op jit(solution)/shard_map/jit(_take)/gather | solution.py:76
  41.5 14.2 %gather_fusion.1 = s32[4096,15]{1,0:T(8,128)} fusion(s32[2048,15]{1,0:T(8,128)S(1)} %copy.43, s32[4096]{0:T(1024)S(1)} %broadcast_clamp_fusion), kind=kCustom, calls=%fused_computation.1 | custom fusion | bytes 507904 | tf_op jit(solution)/shard_map/jit(_take)/gather | solution.py:74
  55.7 2.2 copy.44
  57.9 23.0 %gather_fusion = s32[4096]{0:T(1024)S(1)} fusion(s32[2048]{0:T(1024)S(1)} %copy-done.2, s32[4096]{0:T(1024)S(1)} %broadcast_clamp_fusion), kind=kCustom, calls=%fused_computation | custom fusion | bytes 49152 | tf_op jit(solution)/shard_map/jit(_take)/gather | solution.py:75
  81.0 254.4 %while.14 = (s32[]{:T(128)}, bf16[8,32,512]{2,1,0:T(8,128)(2,1)}, bf16[8,32,512]{2,1,0:T(8,128)(2,1)}, s32[8,512]{1,0:T(8,128)S(1)}, pred[8,512]{1,0:T(8,128)(4,...) while((s32[]{:T(128)}, bf16[8,32,512]{2,1,0:T(8,128)(2,1)}, ...), condition=%wide.region_5.6_spmd.clone.clone, body=%wide.region_4.5_spmd.clone.clone.sunk | while | flops 398523904 | bytes 777833 | solution.py:105
  81.5 27.7 %fusion.138 = bf16[8,32,512]{2,1,0:T(8,128)(2,1)} fusion(bf16[8,32,512]{2,1,0:T(8,128)(2,1)} %get-tuple-element.411, s32[]{:T(128)} %get-tuple-element.409, bf16[32,4096]{1,0:T(8,128)(2,1)S(1)} %get-tuple-element.423, s32[512]{0:T(512)S(1)} %bitcast.172, s32[512]{0:T(512)S(1)} %bitcast.173, s32[512]{0:T(512)S(1)} %bitcast.174, ...), kind=kOutput, calls=%fused_computation.63.clone.1 | convolution fusion | flops 260079616 | bytes 335872 | tf_op jit(solution)/shard_map/while/body/eval_jaxpr/dot_general | solution.py:93
  109.2 2.3 fusion.136
  111.7 27.7 %fusion.138 = bf16[8,32,512]{2,1,0:T(8,128)(2,1)} fusion(bf16[8,32,512]{2,1,0:T(8,128)(2,1)} %get-tuple-element.411, s32[]{:T(128)} %get-tuple-element.409, bf16[32,4096]{1,0:T(8,128)(2,1)S(1)} %get-tuple-element.423, s32[512]{0:T(512)S(1)} %bitcast.172, s32[512]{0:T(512)S(1)} %bitcast.173, s32[512]{0:T(512)S(1)} %bitcast.174, ...), kind=kOutput, calls=%fused_computation.63.clone.1 | convolution fusion | flops 260079616 | bytes 335872 | tf_op jit(solution)/shard_map/while/body/eval_jaxpr/dot_general | solution.py:93
  139.4 2.3 fusion.136
  141.9 27.7 %fusion.138 = bf16[8,32,512]{2,1,0:T(8,128)(2,1)} fusion(bf16[8,32,512]{2,1,0:T(8,128)(2,1)} %get-tuple-element.411, s32[]{:T(128)} %get-tuple-element.409, bf16[32,4096]{1,0:T(8,128)(2,1)S(1)} %get-tuple-element.423, s32[512]{0:T(512)S(1)} %bitcast.172, s32[512]{0:T(512)S(1)} %bitcast.173, s32[512]{0:T(512)S(1)} %bitcast.174, ...), kind=kOutput, calls=%fused_computation.63.clone.1 | convolution fusion | flops 260079616 | bytes 335872 | tf_op jit(solution)/shard_map/while/body/eval_jaxpr/dot_general | solution.py:93
  169.6 2.3 fusion.136
  172.1 27.7 %fusion.138 = bf16[8,32,512]{2,1,0:T(8,128)(2,1)} fusion(bf16[8,32,512]{2,1,0:T(8,128)(2,1)} %get-tuple-element.411, s32[]{:T(128)} %get-tuple-element.409, bf16[32,4096]{1,0:T(8,128)(2,1)S(1)} %get-tuple-element.423, s32[512]{0:T(512)S(1)} %bitcast.172, s32[512]{0:T(512)S(1)} %bitcast.173, s32[512]{0:T(512)S(1)} %bitcast.174, ...), kind=kOutput, calls=%fused_computation.63.clone.1 | convolution fusion | flops 260079616 | bytes 335872 | tf_op jit(solution)/shard_map/while/body/eval_jaxpr/dot_general | solution.py:93
  199.8 2.3 fusion.136
  202.3 27.7 %fusion.138 = bf16[8,32,512]{2,1,0:T(8,128)(2,1)} fusion(bf16[8,32,512]{2,1,0:T(8,128)(2,1)} %get-tuple-element.411, s32[]{:T(128)} %get-tuple-element.409, bf16[32,4096]{1,0:T(8,128)(2,1)S(1)} %get-tuple-element.423, s32[512]{0:T(512)S(1)} %bitcast.172, s32[512]{0:T(512)S(1)} %bitcast.173, s32[512]{0:T(512)S(1)} %bitcast.174, ...), kind=kOutput, calls=%fused_computation.63.clone.1 | convolution fusion | flops 260079616 | bytes 335872 | tf_op jit(solution)/shard_map/while/body/eval_jaxpr/dot_general | solution.py:93
  230.0 2.3 fusion.136
  232.4 27.7 %fusion.138 = bf16[8,32,512]{2,1,0:T(8,128)(2,1)} fusion(bf16[8,32,512]{2,1,0:T(8,128)(2,1)} %get-tuple-element.411, s32[]{:T(128)} %get-tuple-element.409, bf16[32,4096]{1,0:T(8,128)(2,1)S(1)} %get-tuple-element.423, s32[512]{0:T(512)S(1)} %bitcast.172, s32[512]{0:T(512)S(1)} %bitcast.173, s32[512]{0:T(512)S(1)} %bitcast.174, ...), kind=kOutput, calls=%fused_computation.63.clone.1 | convolution fusion | flops 260079616 | bytes 335872 | tf_op jit(solution)/shard_map/while/body/eval_jaxpr/dot_general | solution.py:93
  260.1 2.3 fusion.136
  262.6 27.7 %fusion.138 = bf16[8,32,512]{2,1,0:T(8,128)(2,1)} fusion(bf16[8,32,512]{2,1,0:T(8,128)(2,1)} %get-tuple-element.411, s32[]{:T(128)} %get-tuple-element.409, bf16[32,4096]{1,0:T(8,128)(2,1)S(1)} %get-tuple-element.423, s32[512]{0:T(512)S(1)} %bitcast.172, s32[512]{0:T(512)S(1)} %bitcast.173, s32[512]{0:T(512)S(1)} %bitcast.174, ...), kind=kOutput, calls=%fused_computation.63.clone.1 | convolution fusion | flops 260079616 | bytes 335872 | tf_op jit(solution)/shard_map/while/body/eval_jaxpr/dot_general | solution.py:93
  290.3 2.3 fusion.136
  292.8 27.7 %fusion.138 = bf16[8,32,512]{2,1,0:T(8,128)(2,1)} fusion(bf16[8,32,512]{2,1,0:T(8,128)(2,1)} %get-tuple-element.411, s32[]{:T(128)} %get-tuple-element.409, bf16[32,4096]{1,0:T(8,128)(2,1)S(1)} %get-tuple-element.423, s32[512]{0:T(512)S(1)} %bitcast.172, s32[512]{0:T(512)S(1)} %bitcast.173, s32[512]{0:T(512)S(1)} %bitcast.174, ...), kind=kOutput, calls=%fused_computation.63.clone.1 | convolution fusion | flops 260079616 | bytes 335872 | tf_op jit(solution)/shard_map/while/body/eval_jaxpr/dot_general | solution.py:93
  320.5 2.3 fusion.136
  338.2 1.6 stack.8
  339.8 1.7 pad_maximum_fusion
  341.5 2.7 copy.54
  344.1 4.5 reshape.178
  348.6 11.5 %all-to-all-start = ((bf16[128,2,1024]{2,1,0:T(2,128)(2,1)}), bf16[128,2,1024]{2,1,0:T(2,128)(2,1)S(1)}, u32[]{:S(2)}, u32[]{:S(2)}) async-start(bf16[128,2,1024]{2,1,0:T(2,128)(2,1)} %reshape.178), calls=%async_computation | async-start | bytes 1048576 | tf_op jit(solution)/shard_map/all_to_all | solution.py:109
  360.2 15.3 %all_gather.3 = bf16[128,2048]{1,0:T(8,128)(2,1)S(1)} all-gather(bf16[32,2048]{1,0:T(8,128)(2,1)S(1)} %pad_maximum_fusion.2), channel_id=1, replica_groups=mesh['feat'=4,'trainer'=32] {'feat'}, dimensions={0}, use_global_device_ids=true | all-gather | bytes 655360 | tf_op jit(solution)/shard_map/all_gather | solution.py:12
  377.3 2.0 reshape.179
  379.3 2.9 copy.53
  382.3 1.6 fusion.91
  385.3 1.2 slice.218
  386.5 1.9 slice.221
  388.4 2.7 fusion.81
  391.0 2.7 fusion.78
  395.0 1.9 slice.227
  396.9 3.6 fusion.75
  401.7 2.7 fusion.84
  404.7 3.1 add_convert_fusion.12
  408.8 1.5 copy-done.5
  411.0 1.5 copy-done.7
  412.5 3.5 fusion.53
  416.1 1.7 fusion.66
  418.6 1.3 fusion.94
  420.0 7.0 divide_convert_fusion.1
  427.1 3.1 convert_reduce_fusion.1
  430.2 5.9 fusion.54
  436.1 4.6 fusion.96
  440.7 3.3 fusion.95
  444.0 11.3 %convert_reduce_fusion = (f32[1024]{0:T(1024)S(1)}, bf16[1024,1024]{1,0:T(8,128)(2,1)}) fusion(bf16[1024,1024]{1,0:T(8,128)(2,1)} %copy-done.43, f32[1024,1024]{1,0:T(8,128)} %fusion.54, bf16[512,1024]{1,0:T(8,128)(2,1)S(1)} %get-tuple-element.227, bf16[1024,1024]{1,0:T(8,128)(2,1)S(1)} %copy-done, f32[512]{0:T(512)S(1)} %copy-done.26, ...), kind=kOutput, calls=%fused_computation.87 | convolution fusion | flops 2177891328 | bytes 11566080 | tf_op jit(solution)/shard_map/dot_general | solution.py:26
  455.4 3.0 fusion.90
  458.4 2.3 squeeze.13
  460.7 2.0 convolution_bitcast_fusion.1
  464.8 2.7 convolution_bitcast_fusion
  468.8 108.3 %all-reduce.8.cloned.1.call-done = (f32[1024,1024]{1,0:T(8,128)}, f32[1024,1024]{1,0:T(8,128)}) async-done(((f32[1024,1024]{1,0:T(8,128)}, f32[1024,1024]{1,0:T(8,128)}), (f32[1024,1024]{1,0:T(8,128)}, f32[1024,1024]{1,0:T(8,128)})) %all-reduce.8.cloned.1.call-update) | async-done | bytes 8388624 | tf_op jit(solution)/shard_map/psum | solution.py:153
  577.1 62.9 %psum.53 = f32[1024]{0:T(1024)S(1)} all-reduce(f32[1024]{0:T(1024)S(1)} %get-tuple-element.226), channel_id=1, replica_groups=mesh['feat'=4,'trainer'=32] {'trainer'}, use_global_device_ids=true, to_apply=%region_11.12 | all-reduce | flops 1024 | bytes 8192 | tf_op jit(solution)/shard_map/psum | solution.py:153
  640.0 9.5 %psum.54 = f32[1024]{0:T(1024)} all-reduce(f32[1024]{0:T(1024)S(1)} %psum.53), channel_id=1, replica_groups=mesh['feat'=4,'trainer'=32] {'feat'}, use_global_device_ids=true, to_apply=%region_12.13 | all-reduce | flops 1024 | bytes 8192 | tf_op jit(solution)/shard_map/psum | solution.py:152
  649.5 80.4 %all-reduce.6.cloned.1.call-done = f32[263168]{0:T(1024)} async-done(((f32[263168]{0:T(1024)}), f32[263168]{0:T(1024)}) %all-reduce.6.cloned.1.call-update) | async-done | bytes 1052688 | tf_op jit(solution)/shard_map/psum | solution.py:18
  729.9 1.3 fusion.92
  732.1 1.3 slice.322
  733.4 1.6 constant_dynamic-slice_fusion.3
  735.0 156.3 %all-reduce.10.cloned.1.call-done = (f32[1024,1024]{1,0:T(8,128)}, f32[1024,1024]{1,0:T(8,128)}) async-done(((f32[1024,1024]{1,0:T(8,128)}, f32[1024,1024]{1,0:T(8,128)}), (f32[1024,1024]{1,0:T(8,128)}, f32[1024,1024]{1,0:T(8,128)})) %all-reduce.10.cloned.1.call-update) | async-done | bytes 8388624 | tf_op jit(solution)/shard_map/psum | solution.py:152
  891.4 4.9 copy.71
  896.3 2.0 copy.72
  (163 shorter events, 20.0 us)
Async XLA Ops:
  7.2 419.9 %copy-start = (bf16[1024,1024]{1,0:T(8,128)(2,1)S(1)}, bf16[1024,1024]{1,0:T(8,128)(2,1)}, u32[]{:S(2)}) copy-start(bf16[1024,1024]{1,0:T(8,128)(2,1)} %param.29) | copy-start | bytes 6291460
  8.5 0.7 copy-start.15
  8.6 9.3 %copy-start.1 = (s32[2048]{0:T(1024)S(1)}, s32[2048]{0:T(1024)}, u32[]{:S(2)}) copy-start(s32[2048]{0:T(1024)} %param.20) | copy-start | bytes 24580
  18.0 23.1 %copy-start.14 = (s32[2048,15]{0,1:T(8,128)S(1)}, s32[2048,15]{0,1:T(8,128)}, u32[]{:S(2)}) copy-start(s32[2048,15]{0,1:T(8,128)} %param.18) | copy-start | bytes 368644
  55.7 2.2 copy-start.2
  57.9 23.1 %copy-start.39 = (bf16[32,4096]{1,0:T(8,128)(2,1)S(1)}, bf16[32,4096]{1,0:T(8,128)(2,1)}, u32[]{:S(2)}) copy-start(bf16[32,4096]{1,0:T(8,128)(2,1)} %param.17) | copy-start | bytes 786436
  344.1 16.0 %copy-start.16 = (bf16[32,1024]{1,0:T(8,128)(2,1)S(1)}, bf16[32,1024]{1,0:T(8,128)(2,1)}, u32[]{:S(2)}) copy-start(bf16[32,1024]{1,0:T(8,128)(2,1)} %param.23) | copy-start | bytes 196612
  344.1 16.0 %copy-start.17 = (bf16[32,1024]{1,0:T(8,128)(2,1)S(1)}, bf16[32,1024]{1,0:T(8,128)(2,1)}, u32[]{:S(2)}) copy-start(bf16[32,1024]{1,0:T(8,128)(2,1)} %param.22) | copy-start | bytes 196612
  344.1 31.3 %copy-start.19 = (s32[512]{0:T(512)S(1)}, s32[512]{0:T(512)}, u32[]{:S(2)}) copy-start(s32[512]{0:T(512)} %param.27) | copy-start | bytes 6148
  344.1 32.5 %copy-start.18 = (s32[512,10]{0,1:T(8,128)S(1)}, s32[512,10]{0,1:T(8,128)}, u32[]{:S(2)}) copy-start(s32[512,10]{0,1:T(8,128)} %param.25) | copy-start | bytes 61444
  348.6 28.7 %all-to-all-start = ((bf16[128,2,1024]{2,1,0:T(2,128)(2,1)}), bf16[128,2,1024]{2,1,0:T(2,128)(2,1)S(1)}, u32[]{:S(2)}, u32[]{:S(2)}) async-start(bf16[128,2,1024]{2,1,0:T(2,128)(2,1)} %reshape.178), calls=%async_computation | async-start | bytes 1048576 | tf_op jit(solution)/shard_map/all_to_all | solution.py:109
  360.1 216.9 %all-reduce.8.cloned.1.call-start = ((), (), s32[]{:S(2)}) async-start(), calls=%async_computation.2 | async-start | bytes 16777216 | tf_op jit(solution)/shard_map/psum | solution.py:153
  382.2 1.8 copy-start.3
  388.4 2.7 copy-start.13
  404.6 3.5 copy-start.4
  408.1 2.2 copy-start.5
  408.1 2.2 copy-start.12
  410.3 2.2 copy-start.7
  410.3 2.2 copy-start.40
  412.5 3.5 copy-start.42
  416.0 3.8 copy-start.43
  416.0 2.4 copy-start.37
  418.4 1.4 copy-start.9
  418.4 1.4 copy-start.20
  418.4 1.4 copy-start.21
  418.4 1.5 copy-start.22
  418.4 1.5 copy-start.23
  418.4 1.5 copy-start.24
  418.4 1.5 copy-start.25
  418.4 1.5 copy-start.26
  418.5 1.5 copy-start.27
  418.5 1.5 copy-start.28
  418.5 1.5 copy-start.29
  418.5 1.5 copy-start.30
  418.5 1.5 copy-start.31
  418.5 1.5 copy-start.32
  418.5 1.5 copy-start.33
  418.5 1.5 copy-start.34
  418.5 1.5 copy-start.35
  418.5 1.5 copy-start.36
  420.0 7.1 copy-start.38
  420.0 7.1 copy-start.41
  427.1 3.1 copy-start.11
  436.1 4.6 copy-start.10
  455.3 274.6 %all-reduce.6.cloned.1.call-start = ((), (), s32[]{:S(2)}) async-start(), calls=%async_computation.1 | async-start | bytes 2105344 | tf_op jit(solution)/shard_map/psum | solution.py:18
  464.8 2.8 copy-start.8
  468.7 422.7 %all-reduce.10.cloned.1.call-start = ((), (), s32[]{:S(2)}) async-start(), calls=%async_computation.3 | async-start | bytes 16777216 | tf_op jit(solution)/shard_map/psum | solution.py:152
  891.4 4.9 copy-start.6
Sparse Core Ops, SparseCore 0:
  455.4 121.5 all-reduce.7
  581.8 148.0 all-reduce.5
  732.5 158.8 all-reduce.9
